TPU v7x, 32 devices: a whole 2x2x4 slice. The times are simulated.
32 devices in a mesh: dom: 2 (over y), row: 4 (over z), nbr: 4 (over x, core).
Axes of the slice: x: 2, y: 2, z: 4, core: 2. Of those that a mesh axis runs over, the one named last changes fastest.
Arguments:
- blocks: float32 [24, 12, 128, 128], P(('dom', 'row'), 'nbr'), parts along dimension 0, may hold values from -0.15625 to 0.15625
- partner_ids: int32 [24, 12], P(('dom', 'row'), 'nbr'), parts along dimension 0, may hold values from 0 to 11, as said below
- counts: int32 [24], P(('dom', 'row')), parts along dimension 0, may hold values from 1 to 12, as said below
- start: float32 [3072, 32], P(('dom', 'row')), parts along dimension 0, may hold values from -6 to 6
Outputs:
- basis: float32 [3072, 32], P(('dom', 'row')), parts along dimension 0
- ritz: float32 [64, 32], P('dom'), parts along dimension 0
There are 2 independent parts, one for each index of `dom`. A program takes and returns all parts, laid end to end along the dimension named above; each array names one. Nothing has to cross between parts.
Inputs may be any that keep to these rules, and one draw needn't show every extreme that they name: partner_ids[i,0] == i; slots 1 to counts[i] - 1 hold distinct block columns greater than i; slots from counts[i] on hold i. counts[i] <= min(12, 12 - i); counts[0] == 12.
All inputs are finite; a program needn't handle non-finite values.
Results may differ from a plain program's by a relative error of at most 0.0001.
Values sent between devices are 32-bit elements; how exact they have to be, the bound alone decides.
A program may use at most 64 MiB of HBM per device.

v0:
```python
import jax
import jax.numpy as jnp
from jax import lax
from jax.sharding import PartitionSpec as P

ITERS = 2
HIGH = lax.Precision.HIGHEST


def orthonormal(image, gram, total):
    lower = jnp.linalg.cholesky(gram / total)
    return lax.linalg.triangular_solve(lower, image, left_side=False, lower=True, transpose_a=True)


def body(blocks, partner_ids, counts, start):
    block_rows, slots_here = partner_ids.shape
    block_size = blocks.shape[2]
    columns = start.shape[1]
    row_count = lax.axis_size("row")
    all_blocks = block_rows * row_count
    total = all_blocks * block_size
    first_row = lax.axis_index("row") * block_rows
    rows_here = first_row + jnp.arange(block_rows, dtype=jnp.int32)
    slot_index = lax.axis_index("nbr") * slots_here + jnp.arange(slots_here, dtype=jnp.int32)
    valid = slot_index[None, :] < counts[:, None]
    weight = jnp.where(valid, jnp.where(partner_ids == rows_here[:, None], 0.5, 1.0), 0.0).astype(
        jnp.float32
    )
    targets = jnp.concatenate([partner_ids.reshape(-1), rows_here])
    whole = lax.all_gather(start, "row", axis=0, tiled=True)
    cross = jnp.zeros((columns, columns), jnp.float32)
    prior = start
    for step in range(ITERS):
        tiles = whole.reshape(all_blocks, block_size, columns)
        far = tiles[partner_ids] * weight[:, :, None, None]
        near = lax.dynamic_slice_in_dim(tiles, first_row, block_rows, 0)
        direct = jnp.einsum("ipab,ipbk->iak", blocks, far, precision=HIGH)
        transposed = (
            jnp.einsum("ipab,iak->ipbk", blocks, near, precision=HIGH) * weight[:, :, None, None]
        )
        items = jnp.concatenate(
            [transposed.reshape(block_rows * slots_here, block_size, columns), direct], axis=0
        )
        placed = jnp.zeros((all_blocks, block_size, columns), jnp.float32).at[targets].add(items)
        summed = lax.psum_scatter(
            placed.reshape(total, columns), "row", scatter_dimension=0, tiled=True
        )
        image = lax.psum(summed, "nbr")
        gram, cross = lax.psum(
            (jnp.dot(image.T, image, precision=HIGH), jnp.dot(prior.T, image, precision=HIGH)),
            "row",
        )
        cross = cross / total
        prior = orthonormal(image, gram, total)
        if step + 1 < ITERS:
            whole = lax.all_gather(prior, "row", axis=0, tiled=True)
    return (prior, cross)


def solution(mesh):
    return jax.shard_map(
        body,
        mesh=mesh,
        in_specs=(
            P(("dom", "row"), "nbr", None, None),
            P(("dom", "row"), "nbr"),
            P(("dom", "row")),
            P(("dom", "row"), None),
        ),
        out_specs=(P(("dom", "row"), None), P("dom", None)),
        check_vma=False,
    )
```

profile of v0, /device:TPU:0, one launch (start us, length us, event | category | flops | bytes accessed | tf_op | source)
XLA Modules:
  0.0 162.5 jit_solution(3839742283190382437)
XLA Ops:
  7.2 0.8 concatenate.32
  8.2 15.7 %all_gather.6 = f32[1536,32]{0,1:T(8,128)S(1)} all-gather(f32[384,32]{0,1:T(8,128)} %param.10), channel_id=1, replica_groups=mesh['dom'=2,'row'=4,'nbr'=4] {'row'}, dimensions={0}, use_global_device_ids=true | all-gather | bytes 245760 | tf_op jit(solution)/shard_map/all_gather | solution.py:30
  23.9 0.6 gather_fusion
  24.4 0.6 copy-done.2
  25.2 0.5 convolution_multiply_fusion.1
  25.6 0.8 convolution_bitcast_fusion.3
  26.5 1.1 scatter_fusion
  27.6 0.7 copy_bitcast_fusion.1
  28.4 21.0 %reduce-scatter.3.cloned.1.call-done = f32[384,32]{0,1:T(8,128)} async-done(((f32[1536,32]{0,1:T(8,128)}), f32[384,32]{0,1:T(8,128)}) %reduce-scatter.3.cloned.1.call-update) | async-done | bytes 49168 | tf_op jit(solution)/shard_map/reduce_scatter | solution.py:45
  49.4 11.0 %psum.35 = f32[384,32]{0,1:T(8,128)S(1)} all-reduce(f32[384,32]{0,1:T(8,128)} %reduce-scatter.3.cloned.1.call-done), channel_id=1, replica_groups=mesh['dom'=2,'row'=4,'nbr'=4] {'nbr'}, use_global_device_ids=true, to_apply=%region_2.3 | all-reduce | flops 12288 | bytes 98304 | tf_op jit(solution)/shard_map/psum | solution.py:48
  60.6 15.9 %psum.36 = f32[32,32]{0,1:T(8,128)S(1)} all-reduce(f32[32,32]{0,1:T(8,128)S(1)} %fusion.20), channel_id=1, replica_groups=mesh['dom'=2,'row'=4,'nbr'=4] {'row'}, use_global_device_ids=true, to_apply=%region_3.4 | all-reduce | flops 1024 | bytes 8192 | tf_op jit(solution)/shard_map/psum | solution.py:49
  76.6 2.9 %cholesky.44 = f32[32,32]{1,0:T(8,128)S(1)} custom-call(f32[32,32]{1,0:T(8,128)S(1)} %fusion.13), custom_call_target="Cholesky" | custom-call | tf_op jit(solution)/shard_map/jit(cholesky)/cholesky | solution.py:11
  79.5 0.6 compare_reduce_fusion.1
  80.2 0.7 fusion.8
  80.8 2.4 %custom-call.6 = f32[1,32,32]{1,2,0:T(8,128)S(1)} custom-call(f32[1,32,32]{2,1,0:T(8,128)S(1)} %fusion.8), custom_call_target="InvertDiagBlocksLowerTriangular" | custom-call | tf_op jit(solution)/shard_map/triangular_solve/custom-call.0 | solution.py:12
  83.3 0.3 convolution_bitcast_fusion.2
  83.5 13.6 %all_gather.7 = f32[1536,32]{0,1:T(8,128)S(1)} all-gather(f32[384,32]{0,1:T(8,128)S(1)} %convolution_bitcast_fusion.2), channel_id=1, replica_groups=mesh['dom'=2,'row'=4,'nbr'=4] {'row'}, dimensions={0}, use_global_device_ids=true | all-gather | bytes 245760 | tf_op jit(solution)/shard_map/all_gather | solution.py:56
  97.1 0.6 gather_fusion.1
  97.7 0.5 convolution_multiply_fusion
  98.2 0.8 convolution_bitcast_fusion.1
  99.0 1.1 scatter_fusion.1
  100.1 0.7 copy_bitcast_fusion
  100.8 18.8 %reduce-scatter.5.cloned.1.call-done = f32[384,32]{0,1:T(8,128)} async-done(((f32[1536,32]{0,1:T(8,128)}), f32[384,32]{0,1:T(8,128)}) %reduce-scatter.5.cloned.1.call-update) | async-done | bytes 49168 | tf_op jit(solution)/shard_map/reduce_scatter | solution.py:45
  119.6 11.0 %psum.37 = f32[384,32]{0,1:T(8,128)S(1)} all-reduce(f32[384,32]{0,1:T(8,128)} %reduce-scatter.5.cloned.1.call-done), channel_id=1, replica_groups=mesh['dom'=2,'row'=4,'nbr'=4] {'nbr'}, use_global_device_ids=true, to_apply=%region_8.11 | all-reduce | flops 12288 | bytes 98304 | tf_op jit(solution)/shard_map/psum | solution.py:48
  130.6 0.2 fusion.22
  131.0 16.2 %all-reduce = (f32[32,32]{0,1:T(8,128)S(1)}, f32[32,32]{0,1:T(8,128)S(1)}) all-reduce(f32[32,32]{0,1:T(8,128)S(1)} %fusion.21, f32[32,32]{0,1:T(8,128)S(1)} %fusion.22), channel_id=1, replica_groups=mesh['dom'=2,'row'=4,'nbr'=4] {'row'}, use_global_device_ids=true, to_apply=%region_9.12 | all-reduce | flops 2048 | bytes 16384 | tf_op jit(solution)/shard_map/psum | solution.py:49
  147.3 0.7 copy.37
  148.0 2.9 %cholesky.55 = f32[32,32]{1,0:T(8,128)S(1)} custom-call(f32[32,32]{1,0:T(8,128)S(1)} %fusion.11), custom_call_target="Cholesky" | custom-call | tf_op jit(solution)/shard_map/jit(cholesky)/cholesky | solution.py:11
  151.0 0.6 compare_reduce_fusion
  151.6 0.7 fusion.9
  152.3 2.4 %custom-call.7 = f32[1,32,32]{1,2,0:T(8,128)S(1)} custom-call(f32[1,32,32]{2,1,0:T(8,128)S(1)} %fusion.9), custom_call_target="InvertDiagBlocksLowerTriangular" | custom-call | tf_op jit(solution)/shard_map/triangular_solve/custom-call.0 | solution.py:12
  154.7 0.9 convolution_bitcast_fusion
  (33 shorter events, 1.1 us)
Async XLA Ops:
  7.2 18.0 %copy-start = (f32[3,3,128,128]{3,2,1,0:T(8,128)S(1)}, f32[3,3,128,128]{3,2,1,0:T(8,128)}, u32[]{:S(2)}) copy-start(f32[3,3,128,128]{3,2,1,0:T(8,128)} %param.7) | copy-start | bytes 1769476
  7.2 0.9 copy-start.1
  7.2 42.2 %reduce-scatter.3.cloned.1.call-start = ((), (), s32[]{:S(2)}) async-start(), calls=%async_computation.2 | async-start | bytes 245760 | tf_op jit(solution)/shard_map/reduce_scatter | solution.py:45
  24.4 0.7 copy-start.2
  28.3 91.3 %reduce-scatter.5.cloned.1.call-start = ((), (), s32[]{:S(2)}) async-start(), calls=%async_computation.3 | async-start | bytes 245760 | tf_op jit(solution)/shard_map/reduce_scatter | solution.py:45
Sparse Core Ops, SparseCore 0:
  28.4 20.9 reduce-scatter.2
  100.9 18.6 reduce-scatter.4
where the time goes:
time: 163 us; the launch traced here: 162 us
  blocking collectives  83.4 us (51%)
  waiting for transfers between devices  39.9 us (24%)
  other arithmetic  15.8 us (10%)
  between operations  14.3 us (9%)
  local copies, waits for them, and re-layouts  4.93 us (3%)
  matrix products  4.18 us (3%)
    reduce_scatter x2, waiting for transfers between devices, body(): lax.psum_scatter(placed.reshape(total, columns), 'row', scatter_dimension...  39.8 us
    psum x2, blocking collectives, body(): lax.psum((jnp.dot(image.T, image, precision=HIGH), jnp.dot(prior.T, image...  32.1 us
    psum x2, blocking collectives, body(): image = lax.psum(summed, 'nbr')  22 us
    all_gather x1, blocking collectives, body(): whole = lax.all_gather(start, 'row', axis=0, tiled=True)  15.7 us
    all_gather x1, blocking collectives, body(): whole = lax.all_gather(prior, 'row', axis=0, tiled=True)  13.6 us
    another operation x6, other arithmetic, orthonormal(): lower = jnp.linalg.cholesky(gram / total)  7.19 us
    another operation x4, other arithmetic, orthonormal(): lax.linalg.triangular_solve(lower, image, left_side=False, lower=True, tr...  6.17 us
  transfers between devices with their start and end apart: 2, of which 2 were waited for; matrix products, arithmetic and copies ran while one was open for 0% of the time, Pallas kernels for 0%

commit v1 on v0

--- a/solution.py
+++ b/solution.py
@@ -45,7 +45,7 @@
         summed = lax.psum_scatter(
             placed.reshape(total, columns), "row", scatter_dimension=0, tiled=True
         )
-        image = lax.psum(summed, "nbr")
+        image = jnp.sum(lax.all_gather(summed, "nbr"), axis=0)
         gram, cross = lax.psum(
             (jnp.dot(image.T, image, precision=HIGH), jnp.dot(prior.T, image, precision=HIGH)),
             "row",

time: 163 us -> 152 us (0.933)
  blocking collectives: 83.4 us -> 72.9 us
    psum x2 -> x0, blocking collectives: 22 us -> none  [body(): image = lax.psum(summed, 'nbr')]
    all_gather x0 -> x2, blocking collectives: none -> 11.6 us  [body(): image = jnp.sum(lax.all_gather(summed, 'nbr'), axis=0)]
where the time goes in v1:
time: 152 us
  blocking collectives  72.9 us (48%)
  waiting for transfers between devices  39.3 us (26%)
  other arithmetic  16.8 us (11%)
  between operations  14.3 us (9%)
  local copies, waits for them, and re-layouts  4.33 us (3%)
  matrix products  4.18 us (3%)
    reduce_scatter x2, waiting for transfers between devices, body(): lax.psum_scatter(placed.reshape(total, columns), 'row', scatter_dimension...  39.3 us
    psum x2, blocking collectives, body(): lax.psum((jnp.dot(image.T, image, precision=HIGH), jnp.dot(prior.T, image...  32 us
    all_gather x1, blocking collectives, body(): whole = lax.all_gather(start, 'row', axis=0, tiled=True)  15.7 us
    all_gather x1, blocking collectives, body(): whole = lax.all_gather(prior, 'row', axis=0, tiled=True)  13.6 us
    all_gather x2, blocking collectives, body(): image = jnp.sum(lax.all_gather(summed, 'nbr'), axis=0)  11.6 us
    another operation x6, other arithmetic, orthonormal(): lower = jnp.linalg.cholesky(gram / total)  7.19 us
    another operation x4, other arithmetic, orthonormal(): lax.linalg.triangular_solve(lower, image, left_side=False, lower=True, tr...  6.17 us
  transfers between devices with their start and end apart: 2, of which 2 were waited for; matrix products, arithmetic and copies ran while one was open for 0% of the time, Pallas kernels for 0%

profile of v1, /device:TPU:0, one launch (start us, length us, event | category | flops | bytes accessed | tf_op | source)
XLA Modules:
  0.0 151.8 jit_solution(12798288775264183927)
XLA Ops:
  7.2 0.7 compare_select_fusion
  8.1 15.7 %all_gather.18 = f32[1536,32]{0,1:T(8,128)S(1)} all-gather(f32[384,32]{0,1:T(8,128)} %param.10), channel_id=1, replica_groups=mesh['dom'=2,'row'=4,'nbr'=4] {'row'}, dimensions={0}, use_global_device_ids=true | all-gather | bytes 245760 | tf_op jit(solution)/shard_map/all_gather | solution.py:30
  23.9 0.6 gather_fusion
  24.4 0.6 copy-done.2
  25.2 0.5 convolution_multiply_fusion.1
  25.6 0.8 convolution_bitcast_fusion.3
  26.5 1.1 scatter_fusion
  27.6 0.7 copy_bitcast_fusion.1
  28.4 21.0 %reduce-scatter.3.cloned.1.call-done = f32[384,32]{0,1:T(8,128)} async-done(((f32[1536,32]{0,1:T(8,128)}), f32[384,32]{0,1:T(8,128)}) %reduce-scatter.3.cloned.1.call-update) | async-done | bytes 49168 | tf_op jit(solution)/shard_map/reduce_scatter | solution.py:45
  49.4 5.8 %all-gather = f32[1536,32]{0,1:T(8,128)S(1)} all-gather(f32[384,32]{0,1:T(8,128)} %reduce-scatter.3.cloned.1.call-done), channel_id=2, replica_groups=mesh['dom'=2,'row'=4,'nbr'=4] {'nbr'}, dimensions={0}, use_global_device_ids=true | all-gather | bytes 245760 | tf_op jit(solution)/shard_map/all_gather | solution.py:48
  55.6 15.9 %psum.21 = f32[32,32]{0,1:T(8,128)S(1)} all-reduce(f32[32,32]{0,1:T(8,128)S(1)} %fusion.20), channel_id=1, replica_groups=mesh['dom'=2,'row'=4,'nbr'=4] {'row'}, use_global_device_ids=true, to_apply=%region_3.4 | all-reduce | flops 1024 | bytes 8192 | tf_op jit(solution)/shard_map/psum | solution.py:49
  71.5 2.9 %cholesky.44 = f32[32,32]{1,0:T(8,128)S(1)} custom-call(f32[32,32]{1,0:T(8,128)S(1)} %fusion.13), custom_call_target="Cholesky" | custom-call | tf_op jit(solution)/shard_map/jit(cholesky)/cholesky | solution.py:11
  74.5 0.6 compare_reduce_fusion.1
  75.1 0.7 fusion.8
  75.8 2.4 %custom-call.6 = f32[1,32,32]{1,2,0:T(8,128)S(1)} custom-call(f32[1,32,32]{2,1,0:T(8,128)S(1)} %fusion.8), custom_call_target="InvertDiagBlocksLowerTriangular" | custom-call | tf_op jit(solution)/shard_map/triangular_solve/custom-call.0 | solution.py:12
  78.2 0.3 convolution_bitcast_fusion.2
  78.5 13.6 %all_gather.21 = f32[1536,32]{0,1:T(8,128)S(1)} all-gather(f32[384,32]{0,1:T(8,128)S(1)} %convolution_bitcast_fusion.2), channel_id=1, replica_groups=mesh['dom'=2,'row'=4,'nbr'=4] {'row'}, dimensions={0}, use_global_device_ids=true | all-gather | bytes 245760 | tf_op jit(solution)/shard_map/all_gather | solution.py:56
  92.1 0.6 gather_fusion.1
  92.6 0.5 convolution_multiply_fusion
  93.1 0.8 convolution_bitcast_fusion.1
  93.9 1.1 scatter_fusion.1
  95.0 0.7 copy_bitcast_fusion
  95.7 18.2 %reduce-scatter.5.cloned.1.call-done = f32[384,32]{0,1:T(8,128)} async-done(((f32[1536,32]{0,1:T(8,128)}), f32[384,32]{0,1:T(8,128)}) %reduce-scatter.5.cloned.1.call-update) | async-done | bytes 49168 | tf_op jit(solution)/shard_map/reduce_scatter | solution.py:45
  114.0 5.8 %all-gather.1 = f32[1536,32]{0,1:T(8,128)S(1)} all-gather(f32[384,32]{0,1:T(8,128)} %reduce-scatter.5.cloned.1.call-done), channel_id=3, replica_groups=mesh['dom'=2,'row'=4,'nbr'=4] {'nbr'}, dimensions={0}, use_global_device_ids=true | all-gather | bytes 245760 | tf_op jit(solution)/shard_map/all_gather | solution.py:48
  120.0 0.2 fusion.22
  120.4 16.2 %all-reduce = (f32[32,32]{0,1:T(8,128)S(1)}, f32[32,32]{0,1:T(8,128)S(1)}) all-reduce(f32[32,32]{0,1:T(8,128)S(1)} %fusion.21, f32[32,32]{0,1:T(8,128)S(1)} %fusion.22), channel_id=1, replica_groups=mesh['dom'=2,'row'=4,'nbr'=4] {'row'}, use_global_device_ids=true, to_apply=%region_9.12 | all-reduce | flops 2048 | bytes 16384 | tf_op jit(solution)/shard_map/psum | solution.py:49
  136.7 2.9 %cholesky.55 = f32[32,32]{1,0:T(8,128)S(1)} custom-call(f32[32,32]{1,0:T(8,128)S(1)} %fusion.11), custom_call_target="Cholesky" | custom-call | tf_op jit(solution)/shard_map/jit(cholesky)/cholesky | solution.py:11
  139.6 0.6 compare_reduce_fusion
  140.2 0.7 fusion.9
  140.9 2.4 %custom-call.7 = f32[1,32,32]{1,2,0:T(8,128)S(1)} custom-call(f32[1,32,32]{2,1,0:T(8,128)S(1)} %fusion.9), custom_call_target="InvertDiagBlocksLowerTriangular" | custom-call | tf_op jit(solution)/shard_map/triangular_solve/custom-call.0 | solution.py:12
  143.3 0.9 convolution_bitcast_fusion
  144.2 0.7 copy.49
  (37 shorter events, 1.6 us)
Async XLA Ops:
  7.2 18.0 %copy-start = (f32[3,3,128,128]{3,2,1,0:T(8,128)S(1)}, f32[3,3,128,128]{3,2,1,0:T(8,128)}, u32[]{:S(2)}) copy-start(f32[3,3,128,128]{3,2,1,0:T(8,128)} %param.7) | copy-start | bytes 1769476
  7.2 42.2 %reduce-scatter.3.cloned.1.call-start = ((), (), s32[]{:S(2)}) async-start(), calls=%async_computation.2 | async-start | bytes 245760 | tf_op jit(solution)/shard_map/reduce_scatter | solution.py:45
  7.2 0.8 copy-start.1
  24.4 0.7 copy-start.2
  28.3 85.7 %reduce-scatter.5.cloned.1.call-start = ((), (), s32[]{:S(2)}) async-start(), calls=%async_computation.3 | async-start | bytes 245760 | tf_op jit(solution)/shard_map/reduce_scatter | solution.py:45
Sparse Core Ops, SparseCore 0:
  28.5 20.9 reduce-scatter.2
  95.9 18.0 reduce-scatter.4
